TPU v7x, 32 devices: a whole 2x2x4 slice. The times are simulated.
32 devices in a mesh: tok: 8 (over z, x), col: 4 (over y, core).
Axes of the slice: x: 2, y: 2, z: 4, core: 2. Of those that a mesh axis runs over, the one named last changes fastest.
Arguments:
- tokens: bfloat16 [2560, 4096], P('tok', 'col'), may hold values from -16 to 16
- w_query: bfloat16 [4096, 2048], P(None, 'col'), may hold values from -0.09375 to 0.09375
- w_key: bfloat16 [4096, 512], P(None, 'col'), may hold values from -0.09375 to 0.09375
- w_value: bfloat16 [4096, 512], P(None, 'col'), may hold values from -0.09375 to 0.09375
- w_out: bfloat16 [2048, 4096], P('col'), may hold values from -0.125 to 0.125
- block_ids: int32 [16, 40, 16], P('col', 'tok'), may hold values from 0 to 39, as said below
- block_counts: int32 [16, 40], P('col', 'tok'), may hold values from 1 to 16, as said below
Outputs:
- mixed: bfloat16 [2560, 4096], P('tok', 'col')
Inputs may be any that keep to these rules, and one draw needn't show every extreme that they name: block_ids[h, b, 0] = b; the slots below block_counts[h, b] hold distinct blocks none after b; later slots hold block numbers that are not read. block_counts[h, b] <= b + 1; densities differ from head to head, and some row of some head uses all 16 slots.
All inputs are finite; a program needn't handle non-finite values.
Results may differ from a plain program's by a relative error of at most 0.012.
Values may be sent and summed in bfloat16 or wider, within the bound.
No kernel may reach another device: no remote copies, remote signals or barrier semaphores. Data moves between devices by JAX's collectives and lax.ppermute only.
A program may use at most 64 MiB of HBM per device.

v0:
```python
import jax
import jax.numpy as jnp
from jax import lax
from jax.sharding import PartitionSpec as P

HEAD_SIZE = 128
BLK = 64
NSEL = 16
rope_base = 500000.0


def rotate(field, positions):
    half = field.shape[-1] // 2
    freq = rope_base ** (-jnp.arange(half, dtype=jnp.float32) / half)
    angle = positions[:, None] * freq[None, :]
    cosine = jnp.cos(angle)[:, None, :]
    sine = jnp.sin(angle)[:, None, :]
    first = field[..., :half]
    second = field[..., half:]
    return jnp.concatenate(
        [first * cosine - second * sine, second * cosine + first * sine], axis=-1
    )


def on_device(tokens, w_query, w_key, w_value, w_out, block_ids, block_counts):
    tok_rows = tokens.shape[0]
    head_local = w_query.shape[1] // HEAD_SIZE
    kv_local = w_key.shape[1] // HEAD_SIZE
    group_size = head_local // kv_local
    blocks_dev = block_ids.shape[1]
    piece = lax.all_gather(tokens, "col", axis=1, tiled=True)
    width = piece.shape[1]

    def product(weight):
        return jnp.dot(piece, weight, preferred_element_type=jnp.float32)

    query_raw = product(w_query)
    key_raw = product(w_key)
    value_raw = product(w_value)
    tok_place = lax.axis_index("tok")
    query_index = tok_place * tok_rows + jnp.arange(tok_rows, dtype=jnp.int32)
    positions = query_index.astype(jnp.float32)
    query_rows = rotate(query_raw.reshape(tok_rows, head_local, HEAD_SIZE), positions).astype(
        jnp.bfloat16
    )
    keys = rotate(key_raw.reshape(tok_rows, kv_local, HEAD_SIZE), positions).astype(jnp.bfloat16)
    values = value_raw.astype(jnp.bfloat16).reshape(tok_rows, kv_local, HEAD_SIZE)
    grouped = query_rows.reshape(tok_rows, kv_local, group_size, HEAD_SIZE)
    live = jnp.arange(NSEL, dtype=jnp.int32)[None, None, :] < block_counts[:, :, None]
    last_query = tok_place * tok_rows + tok_rows - 1
    start_state = (
        jnp.full((head_local, tok_rows), -1e30, jnp.float32),
        jnp.zeros((head_local, tok_rows), jnp.float32),
        jnp.zeros((head_local, tok_rows, HEAD_SIZE), jnp.float32),
    )
    key_part = lax.all_gather(keys, "tok", axis=0, tiled=True)
    value_part = lax.all_gather(values, "tok", axis=0, tiled=True)
    amount = key_part.shape[0]
    width = 512
    key_blocks = key_part.reshape(amount // width, width, kv_local, HEAD_SIZE)
    value_blocks = value_part.reshape(amount // width, width, kv_local, HEAD_SIZE)
    offsets = jnp.arange(amount // width, dtype=jnp.int32) * width

    def one_block(state, inputs):
        key_block, value_block, offset = inputs

        def compute(inner_state):
            highest, total, summed_weights = inner_state
            key_index = offset + jnp.arange(width, dtype=jnp.int32)
            key_group = key_index // BLK
            hit = jnp.any(
                (block_ids[:, :, :, None] == key_group[None, None, None, :]) & live[..., None],
                axis=2,
            )
            allowed = jnp.broadcast_to(hit[:, :, None, :], (head_local, blocks_dev, BLK, width))
            allowed = allowed.reshape(head_local, tok_rows, width)
            allowed = allowed & (key_index[None, None, :] <= query_index[None, :, None])
            logit_scores = jnp.einsum(
                "tcgd,kcd->cgtk", grouped, key_block, preferred_element_type=jnp.float32
            )
            logit_scores = logit_scores.reshape(head_local, tok_rows, width) * HEAD_SIZE ** (-0.5)
            masked = jnp.where(allowed, logit_scores, -1e30)
            fresh = jnp.maximum(highest, jnp.max(masked, axis=-1))
            decay = jnp.exp(highest - fresh)
            weights = jnp.where(allowed, jnp.exp(masked - fresh[..., None]), 0.0)
            total = total * decay + jnp.sum(weights, axis=-1)
            rounded_scores = weights.astype(jnp.bfloat16).reshape(
                kv_local, group_size, tok_rows, width
            )
            added = jnp.einsum(
                "cgtk,kcd->cgtd", rounded_scores, value_block, preferred_element_type=jnp.float32
            )
            summed_weights = summed_weights * decay[..., None] + added.reshape(
                head_local, tok_rows, HEAD_SIZE
            )
            return (fresh, total, summed_weights)

        return (
            lax.cond(offset > last_query, lambda inner_state: inner_state, compute, state),
            None,
        )

    result, _ = lax.scan(one_block, start_state, (key_blocks, value_blocks, offsets))
    highest, total, summed_weights = result
    attended = jnp.transpose((summed_weights / total[..., None]).astype(jnp.bfloat16), (1, 0, 2))
    flat = attended.reshape(tok_rows, head_local * HEAD_SIZE)
    summed_out = lax.psum_scatter(
        lax.dot_general(
            w_out, flat, (((0,), (1,)), ((), ())), preferred_element_type=jnp.float32
        ).astype(jnp.bfloat16),
        "col",
        scatter_dimension=0,
        tiled=True,
    ).astype(jnp.float32)
    return jnp.transpose(summed_out).astype(jnp.bfloat16)


def solution(mesh):
    in_specs = (
        P("tok", "col"),
        P(None, "col"),
        P(None, "col"),
        P(None, "col"),
        P("col", None),
        P("col", "tok", None),
        P("col", "tok"),
    )
    out_specs = P("tok", "col")
    return jax.shard_map(
        on_device, mesh=mesh, in_specs=in_specs, out_specs=out_specs, check_vma=False
    )
```

profile of v0, /device:TPU:0, one launch (start us, length us, event | category | flops | bytes accessed | tf_op | source)
XLA Modules:
  0.0 185.4 jit_solution(4791514653528160586)
XLA Ops:
  6.5 0.0 copy-start
  6.5 0.0 all-gather.3.cloned.1.call-start
  6.5 0.7 all-gather.3.cloned.1.call-update
  7.3 0.0 reduce-scatter.2.cloned.1.call-start
  7.3 0.7 copy.25
  8.0 0.6 multiply_cosine_fusion
  8.7 28.5 %all-gather.3.cloned.1.call-done = bf16[320,4096]{1,0:T(8,128)(2,1)} async-done(((bf16[320,1024]{1,0:T(8,128)(2,1)}), bf16[320,4096]{1,0:T(8,128)(2,1)}) %all-gather.3.cloned.1.call-update) | async-done | bytes 2621456 | tf_op jit(solution)/shard_map/all_gather | solution.py:31
  37.2 4.5 %fusion.43 = f32[320,512]{1,0:T(8,128)S(1)} fusion(bf16[320,4096]{1,0:T(8,128)(2,1)} %all-gather.3.cloned.1.call-done, bf16[4096,512]{1,0:T(8,128)(2,1)} %param.12), kind=kOutput, calls=%fused_computation.67 | convolution fusion | flops 1342177280 | bytes 7471104 | tf_op jit(solution)/shard_map/dot_general | solution.py:35
  41.7 0.2 reshape.338
  41.9 0.0 copy-start.1
  41.9 0.4 fusion.42
  42.3 0.0 copy-done
  42.3 1.3 copy-done.1
  43.7 0.0 copy-start.2
  43.7 0.8 convolution_bitcast_fusion
  44.5 0.7 fusion.39
  45.2 0.1 pad_maximum_fusion.1
  45.3 31.9 %all_gather.10 = bf16[2560,1,128]{2,0,1:T(8,128)(2,1)S(1)} all-gather(bf16[320,1,128]{2,0,1:T(8,128)(2,1)S(1)} %pad_maximum_fusion.1), channel_id=1, replica_groups=mesh['tok'=8,'col'=4] {'tok'}, dimensions={0}, use_global_device_ids=true | all-gather | bytes 737280 | tf_op jit(solution)/shard_map/all_gather | solution.py:56
  77.3 0.0 copy-done.2
  77.3 0.8 convolution_convert_fusion.1
  78.1 0.0 copy-start.3
  78.2 31.4 %all-gather = bf16[2560,128]{1,0:T(8,128)(2,1)S(1)} all-gather(bf16[320,128]{1,0:T(8,128)(2,1)S(1)} %convolution_convert_fusion.1), channel_id=2, replica_groups=mesh['tok'=8,'col'=4] {'tok'}, dimensions={0}, use_global_device_ids=true | all-gather | bytes 737280 | tf_op jit(solution)/shard_map/all_gather | solution.py:57
  109.6 0.2 fusion.29
  109.7 0.2 pad_maximum_fusion
  110.0 0.0 copy-done.3
  110.0 11.1 %while.15 = (s32[]{:T(128)}, f32[4,320]{1,0:T(4,128)S(1)}, f32[4,320]{1,0:T(4,128)S(1)}, f32[4,320,128]{2,1,0:T(8,128)S(1)}, s32[5]{0:T(128)S(1)}, /*index=5*/s3...) while((s32[]{:T(128)}, f32[4,320]{1,0:T(4,128)S(1)}, ...), condition=%wide.region_6.7_spmd.clone, body=%wide.region_0.6_spmd.clone.sunk | while | flops 347014272 | bytes 13164303 | solution.py:103
  110.0 0.6 dynamic_slice.33
  111.3 4.4 %conditional.3 = (f32[4,320]{1,0:T(4,128)S(1)}, f32[4,320]{1,0:T(4,128)S(1)}, f32[4,320,128]{2,1,0:T(8,128)S(1)}) conditional(s32[]{:T(128)} %convert_element_type.74, (s32[4,5,16]{2,1,0:T(8,128)S(1)}, s32[]{:T(128)}, s32[4,5,16]{2,1,0:T(8,128)S(1)}, s32[]{:T(128)}, bf16[5,512,1,128]{3,1,2,0:T(8,128)(2,1)S(1)}, /*index=5*/s32[]{:T(128)}, ...), branch_computations={%region_1.4_spmd, %region_5.5_spmd} | conditional | flops 347014272 | bytes 13151224 | solution.py:99
  111.3 0.6 add_select_fusion
  112.0 0.1 broadcast_compare_fusion.1
  112.0 0.3 and_reduce_fusion
  112.3 0.2 broadcast_in_dim.4
  112.5 0.2 broadcast_compare_fusion
  112.7 0.8 fusion.4
  113.5 1.1 fusion.6
  114.6 1.0 fusion.11
  115.7 0.6 dynamic_slice.33
  117.0 0.6 dynamic_slice.33
  118.4 0.6 dynamic_slice.33
  119.7 0.6 dynamic_slice.33
  121.1 5.3 %fusion.28 = bf16[4096,320]{0,1:T(8,128)(2,1)} fusion(bf16[512,4096]{1,0:T(8,128)(2,1)} %param.15, f32[4,320,128]{2,1,0:T(8,128)S(1)} %get-tuple-element.165, f32[4,320]{1,0:T(4,128)S(1)} %get-tuple-element.166), kind=kOutput, calls=%fused_computation.38 | convolution fusion | flops 1343815680 | bytes 7476224 | tf_op jit(solution)/shard_map/dot_general | solution.py:108
  126.4 0.0 reduce-scatter.2.cloned.1.call-update
  126.4 52.1 %reduce-scatter.2.cloned.1.call-done = bf16[1024,320]{0,1:T(8,128)(2,1)} async-done(((bf16[4096,320]{0,1:T(8,128)(2,1)}), bf16[1024,320]{0,1:T(8,128)(2,1)}) %reduce-scatter.2.cloned.1.call-update) | async-done | bytes 655376 | tf_op jit(solution)/shard_map/reduce_scatter | solution.py:107
  (32 shorter events, 0.3 us)
Async XLA Ops:
  6.5 35.8 %copy-start = (bf16[4096,128]{1,0:T(8,128)(2,1)S(1)}, bf16[4096,128]{1,0:T(8,128)(2,1)}, u32[]{:S(2)}) copy-start(bf16[4096,128]{1,0:T(8,128)(2,1)} %param.13) | copy-start | bytes 3145732
  6.5 30.6 %all-gather.3.cloned.1.call-start = ((), (), s32[]{:S(2)}) async-start(), calls=%async_computation.1 | async-start | bytes 3276800 | tf_op jit(solution)/shard_map/all_gather | solution.py:31
  7.3 171.3 %reduce-scatter.2.cloned.1.call-start = ((), (), s32[]{:S(2)}) async-start(), calls=%async_computation.2 | async-start | bytes 3276800 | tf_op jit(solution)/shard_map/reduce_scatter | solution.py:107
  41.9 1.7 copy-start.1
  43.7 33.6 %copy-start.2 = (bf16[4096,128]{1,0:T(8,128)(2,1)S(1)}, bf16[4096,128]{1,0:T(8,128)(2,1)}, u32[]{:S(2)}) copy-start(bf16[4096,128]{1,0:T(8,128)(2,1)} %param.14) | copy-start | bytes 3145732
  78.1 31.9 %copy-start.3 = (s32[4,5]{1,0:T(4,128)S(1)}, s32[4,5]{1,0:T(4,128)}, u32[]{:S(2)}) copy-start(s32[4,5]{1,0:T(4,128)} %param.17) | copy-start | bytes 244
Sparse Core Ops, SparseCore 0:
  8.9 28.2 all-gather.2
  126.5 51.9 reduce-scatter.1
where the time goes:
time: 186 us; the launch traced here: 185 us
  waiting for transfers between devices  81.4 us (44%)
  blocking collectives  63.3 us (34%)
  between operations  13.5 us (7%)
  matrix products  13.4 us (7%)
  local copies, waits for them, and re-layouts  6.13 us (3%)
  other arithmetic  4.08 us (2%)
  loops' own time  3.5 us (2%)
    reduce_scatter x1, waiting for transfers between devices, on_device(): lax.psum_scatter(lax.dot_general(w_out, flat, (((0,), (1,)), ((), ())), p...  52.1 us
    all_gather x1, blocking collectives, on_device(): key_part = lax.all_gather(keys, 'tok', axis=0, tiled=True)  31.9 us
    all_gather x1, blocking collectives, on_device(): value_part = lax.all_gather(values, 'tok', axis=0, tiled=True)  31.4 us
    all_gather x1, waiting for transfers between devices, on_device(): piece = lax.all_gather(tokens, 'col', axis=1, tiled=True)  28.5 us
    dot_general x3, matrix products, product(): return jnp.dot(piece, weight, preferred_element_type=jnp.float32)  6.19 us
    dot_general x1, matrix products, on_device(): lax.dot_general(w_out, flat, (((0,), (1,)), ((), ())), preferred_element_...  5.31 us
  transfers between devices with their start and end apart: 2, of which 2 were waited for; matrix products, arithmetic and copies ran while one was open for 1% of the time, Pallas kernels for 0%

commit v1 on v0

--- a/solution.py
+++ b/solution.py
@@ -23,6 +23,23 @@
 
 
 def on_device(tokens, w_query, w_key, w_value, w_out, block_ids, block_counts):
+
+    def note_slots_for(mine_x):
+        spare = lax.axis_size("tok")
+        state_now = lax.axis_index("tok")
+        carry_out, built, v_now = (spare, state_now, mine_x.shape[0])
+        inter = range(carry_out)
+        d_next = map(lambda ix: (ix, (ix + 1) % carry_out), inter)
+        inbox = list(d_next)
+        val2 = jnp.zeros((*mine_x.shape[:0], carry_out * v_now, *mine_x.shape[1:]), mine_x.dtype)
+        side_arr = mine_x
+        for h in range(carry_out):
+            new = (built - h) % carry_out
+            val2 = lax.dynamic_update_slice_in_dim(val2, side_arr, new * v_now, axis=0)
+            if h < carry_out - 1:
+                side_arr = lax.ppermute(side_arr, axis_name="tok", perm=inbox)
+        return val2
+
     tok_rows = tokens.shape[0]
     head_local = w_query.shape[1] // HEAD_SIZE
     kv_local = w_key.shape[1] // HEAD_SIZE
@@ -53,7 +70,7 @@
         jnp.zeros((head_local, tok_rows), jnp.float32),
         jnp.zeros((head_local, tok_rows, HEAD_SIZE), jnp.float32),
     )
-    key_part = lax.all_gather(keys, "tok", axis=0, tiled=True)
+    key_part = note_slots_for(keys)
     value_part = lax.all_gather(values, "tok", axis=0, tiled=True)
     amount = key_part.shape[0]
     width = 512

time: 186 us -> 197 us (1.059)
  waiting for transfers between devices: 81.4 us -> 117 us
  blocking collectives: 63.3 us -> 31.8 us
  starting transfers between devices: 0.04 us -> 2.1 us
  local copies, waits for them, and re-layouts: 6.13 us -> 8.16 us
    ppermute x0 -> x7, waiting for transfers between devices: none -> 41.5 us  [note_slots_for(): side_arr = lax.ppermute(side_arr, axis_name='tok', perm=inbox)]
    all_gather x1 -> x0, blocking collectives: 31.9 us -> none  [on_device(): key_part = lax.all_gather(keys, 'tok', axis=0, tiled=True)]
    reduce_scatter x1, waiting for transfers between devices: 52.1 us -> 47.6 us  [on_device(): lax.psum_scatter(lax.dot_general(w_out, flat, (((0,), (1,)), ((), ())), p...]
    ppermute x0 -> x7, starting transfers between devices: none -> 2.06 us  [note_slots_for(): side_arr = lax.ppermute(side_arr, axis_name='tok', perm=inbox)]
    dot_general x3, matrix products: 6.19 us -> 8.16 us  [product(): return jnp.dot(piece, weight, preferred_element_type=jnp.float32)]
  transfers between devices with their start and end apart: 2 -> 9, of which waited for: 2 -> 8; matrix products, arithmetic and copies ran while one was open for 1% -> 5% of each run, Pallas kernels for 0% -> 0%
where the time goes in v1:
time: 197 us
  waiting for transfers between devices  117 us (59%)
  blocking collectives  31.8 us (16%)
  matrix products  15.3 us (8%)
  between operations  13.7 us (7%)
  local copies, waits for them, and re-layouts  8.16 us (4%)
  other arithmetic  4.87 us (2%)
  loops' own time  3.61 us (2%)
  starting transfers between devices  2.1 us (1%)
    reduce_scatter x1, waiting for transfers between devices, on_device(): lax.psum_scatter(lax.dot_general(w_out, flat, (((0,), (1,)), ((), ())), p...  47.6 us
    ppermute x7, waiting for transfers between devices, note_slots_for(): side_arr = lax.ppermute(side_arr, axis_name='tok', perm=inbox)  41.5 us
    all_gather x1, blocking collectives, on_device(): value_part = lax.all_gather(values, 'tok', axis=0, tiled=True)  31.8 us
    all_gather x1, waiting for transfers between devices, on_device(): piece = lax.all_gather(tokens, 'col', axis=1, tiled=True)  27.6 us
    dot_general x3, matrix products, product(): return jnp.dot(piece, weight, preferred_element_type=jnp.float32)  8.16 us
    dot_general x1, matrix products, on_device(): lax.dot_general(w_out, flat, (((0,), (1,)), ((), ())), preferred_element_...  5.27 us
  transfers between devices with their start and end apart: 9, of which 8 were waited for; matrix products, arithmetic and copies ran while one was open for 5% of the time, Pallas kernels for 0%

profile of v1, /device:TPU:0, one launch (start us, length us, event | category | flops | bytes accessed | tf_op | source)
XLA Modules:
  0.0 197.0 jit_solution(11368420216935468100)
XLA Ops:
  6.5 0.7 all-gather.3.cloned.1.call-update
  7.3 0.0 reduce-scatter.2.cloned.1.call-start
  7.5 0.7 copy.23
  8.2 1.4 multiply_cosine_fusion
  9.6 27.6 %all-gather.3.cloned.1.call-done = bf16[320,4096]{1,0:T(8,128)(2,1)} async-done(((bf16[320,1024]{1,0:T(8,128)(2,1)}), bf16[320,4096]{1,0:T(8,128)(2,1)}) %all-gather.3.cloned.1.call-update) | async-done | bytes 2621456 | tf_op jit(solution)/shard_map/all_gather | solution.py:48
  37.2 2.7 %convolution_bitcast_fusion = f32[320,1,128]{2,0,1:T(8,128)S(1)} fusion(bf16[320,4096]{1,0:T(8,128)(2,1)} %all-gather.3.cloned.1.call-done, bf16[4096,128]{1,0:T(8,128)(2,1)S(1)} %copy-done), kind=kOutput, calls=%fused_computation.39 | convolution fusion | flops 335544320 | bytes 3833856 | tf_op jit(solution)/shard_map/dot_general | solution.py:52
  39.9 0.7 fusion.39
  40.6 0.1 broadcast_in_dim.23
  40.7 0.1 constant_dynamic-update-slice_fusion.7
  40.9 1.5 collective-permute-start
  42.4 4.6 %fusion.43 = f32[320,512]{1,0:T(8,128)} fusion(bf16[320,4096]{1,0:T(8,128)(2,1)S(1)} %copy-done.1, bf16[4096,512]{1,0:T(8,128)(2,1)} %param.12), kind=kOutput, calls=%fused_computation.75 | convolution fusion | flops 1342177280 | bytes 7471104 | tf_op jit(solution)/shard_map/dot_general | solution.py:52
  47.0 1.4 reshape.338
  48.4 0.4 fusion.42
  48.8 1.3 copy-done.2
  50.1 0.8 convolution_convert_fusion.1
  51.0 31.8 %all-gather = bf16[2560,128]{1,0:T(8,128)(2,1)S(1)} all-gather(bf16[320,128]{1,0:T(8,128)(2,1)S(1)} %convolution_convert_fusion.1), channel_id=2, replica_groups=mesh['tok'=8,'col'=4] {'tok'}, dimensions={0}, use_global_device_ids=true | all-gather | bytes 737280 | tf_op jit(solution)/shard_map/all_gather | solution.py:74
  82.8 0.2 fusion.29
  83.0 0.2 pad_maximum_fusion
  83.2 0.5 collective-permute-start.1
  83.7 0.9 constant_dynamic-update-slice_fusion.6
  84.6 5.9 %collective-permute-done.1 = bf16[320,1,128]{2,0,1:T(8,128)(2,1)S(1)} collective-permute-done((bf16[320,1,128]{2,0,1:T(8,128)(2,1)}, bf16[320,1,128]{2,0,1:T(8,128)(2,1)S(1)}, u32[]{:S(2)}, u32[]{:S(2)}) %collective-permute-start.1) | collective-permute-done | bytes 81952 | tf_op jit(solution)/shard_map/ppermute | solution.py:40
  90.6 7.1 %collective-permute-done.2 = bf16[320,1,128]{2,0,1:T(8,128)(2,1)S(1)} collective-permute-done((bf16[320,1,128]{2,0,1:T(8,128)(2,1)S(1)}, bf16[320,1,128]{2,0,1:T(8,128)(2,1)S(1)}, u32[]{:S(2)}, u32[]{:S(2)}) %collective-permute-start.2) | collective-permute-done | bytes 81952 | tf_op jit(solution)/shard_map/ppermute | solution.py:40
  97.7 0.0 collective-permute-start.3
  97.7 7.1 %collective-permute-done.3 = bf16[320,1,128]{2,0,1:T(8,128)(2,1)S(1)} collective-permute-done((bf16[320,1,128]{2,0,1:T(8,128)(2,1)S(1)}, bf16[320,1,128]{2,0,1:T(8,128)(2,1)S(1)}, u32[]{:S(2)}, u32[]{:S(2)}) %collective-permute-start.3) | collective-permute-done | bytes 81952 | tf_op jit(solution)/shard_map/ppermute | solution.py:40
  104.8 0.0 collective-permute-start.4
  104.9 7.1 %collective-permute-done.4 = bf16[320,1,128]{2,0,1:T(8,128)(2,1)S(1)} collective-permute-done((bf16[320,1,128]{2,0,1:T(8,128)(2,1)S(1)}, bf16[320,1,128]{2,0,1:T(8,128)(2,1)S(1)}, u32[]{:S(2)}, u32[]{:S(2)}) %collective-permute-start.4) | collective-permute-done | bytes 81952 | tf_op jit(solution)/shard_map/ppermute | solution.py:40
  112.0 0.0 collective-permute-start.5
  112.0 7.1 %collective-permute-done.5 = bf16[320,1,128]{2,0,1:T(8,128)(2,1)S(1)} collective-permute-done((bf16[320,1,128]{2,0,1:T(8,128)(2,1)S(1)}, bf16[320,1,128]{2,0,1:T(8,128)(2,1)S(1)}, u32[]{:S(2)}, u32[]{:S(2)}) %collective-permute-start.5) | collective-permute-done | bytes 81952 | tf_op jit(solution)/shard_map/ppermute | solution.py:40
  119.1 0.0 collective-permute-start.6
  119.1 7.1 %collective-permute-done.6 = bf16[320,1,128]{2,0,1:T(8,128)(2,1)S(1)} collective-permute-done((bf16[320,1,128]{2,0,1:T(8,128)(2,1)S(1)}, bf16[320,1,128]{2,0,1:T(8,128)(2,1)S(1)}, u32[]{:S(2)}, u32[]{:S(2)}) %collective-permute-start.6) | collective-permute-done | bytes 81952 | tf_op jit(solution)/shard_map/ppermute | solution.py:40
  126.4 10.9 %while.15 = (s32[]{:T(128)}, f32[4,320]{1,0:T(4,128)S(1)}, f32[4,320]{1,0:T(4,128)S(1)}, f32[4,320,128]{2,1,0:T(8,128)S(1)}, s32[5]{0:T(128)S(1)}, /*index=5*/s3...) while((s32[]{:T(128)}, f32[4,320]{1,0:T(4,128)S(1)}, ...), condition=%wide.region_6.7_spmd.clone, body=%wide.region_0.6_spmd.clone.sunk | while | flops 347014272 | bytes 13164303 | solution.py:120
  126.4 0.6 dynamic_slice.33
  127.6 4.4 %conditional.3 = (f32[4,320]{1,0:T(4,128)S(1)}, f32[4,320]{1,0:T(4,128)S(1)}, f32[4,320,128]{2,1,0:T(8,128)S(1)}) conditional(s32[]{:T(128)} %convert_element_type.74, (s32[4,5,16]{2,1,0:T(8,128)S(1)}, s32[]{:T(128)}, s32[4,5,16]{2,1,0:T(8,128)S(1)}, s32[]{:T(128)}, bf16[5,512,1,128]{3,1,2,0:T(8,128)(2,1)S(1)}, /*index=5*/s32[]{:T(128)}, ...), branch_computations={%region_1.4_spmd, %region_5.5_spmd} | conditional | flops 347014272 | bytes 13151224 | solution.py:116
  127.6 0.7 add_select_fusion
  128.3 0.1 broadcast_compare_fusion.1
  128.4 0.3 and_reduce_fusion
  128.6 0.2 broadcast_in_dim.4
  128.8 0.2 broadcast_compare_fusion
  129.0 0.8 fusion.4
  129.8 1.1 fusion.6
  131.0 1.0 fusion.11
  132.0 0.6 dynamic_slice.33
  133.4 0.6 dynamic_slice.33
  134.7 0.6 dynamic_slice.33
  136.0 0.6 dynamic_slice.33
  137.3 5.3 %fusion.28 = bf16[4096,320]{0,1:T(8,128)(2,1)} fusion(bf16[512,4096]{1,0:T(8,128)(2,1)} %param.15, f32[4,320,128]{2,1,0:T(8,128)S(1)} %get-tuple-element.165, f32[4,320]{1,0:T(4,128)S(1)} %get-tuple-element.166), kind=kOutput, calls=%fused_computation.38 | convolution fusion | flops 1343815680 | bytes 7476224 | tf_op jit(solution)/shard_map/dot_general | solution.py:125
  142.6 0.0 reduce-scatter.2.cloned.1.call-update
  142.6 47.6 %reduce-scatter.2.cloned.1.call-done = bf16[1024,320]{0,1:T(8,128)(2,1)} async-done(((bf16[4096,320]{0,1:T(8,128)(2,1)}), bf16[1024,320]{0,1:T(8,128)(2,1)}) %reduce-scatter.2.cloned.1.call-update) | async-done | bytes 655376 | tf_op jit(solution)/shard_map/reduce_scatter | solution.py:124
  (54 shorter events, 0.4 us)
Async XLA Ops:
  6.5 30.7 %copy-start = (bf16[4096,128]{1,0:T(8,128)(2,1)S(1)}, bf16[4096,128]{1,0:T(8,128)(2,1)}, u32[]{:S(2)}) copy-start(bf16[4096,128]{1,0:T(8,128)(2,1)} %param.13) | copy-start | bytes 3145732
  6.5 30.6 %all-gather.3.cloned.1.call-start = ((), (), s32[]{:S(2)}) async-start(), calls=%async_computation.1 | async-start | bytes 3276800 | tf_op jit(solution)/shard_map/all_gather | solution.py:48
  7.3 182.9 %reduce-scatter.2.cloned.1.call-start = ((), (), s32[]{:S(2)}) async-start(), calls=%async_computation.2 | async-start | bytes 3276800 | tf_op jit(solution)/shard_map/reduce_scatter | solution.py:124
  37.2 5.2 %copy-start.1 = (bf16[320,4096]{1,0:T(8,128)(2,1)S(1)}, bf16[320,4096]{1,0:T(8,128)(2,1)}, u32[]{:S(2)}) copy-start(bf16[320,4096]{1,0:T(8,128)(2,1)} %all-gather.3.cloned.1.call-done) | copy-start | bytes 7864324
  40.9 42.3 %collective-permute-start = (bf16[320,1,128]{2,0,1:T(8,128)(2,1)S(1)}, bf16[320,1,128]{2,0,1:T(8,128)(2,1)}, u32[]{:S(2)}, u32[]{:S(2)}) collective-permute-start(bf16[320,1,128]{2,0,1:T(8,128)(2,1)S(1)} %get-tuple-element.268), channel_id=1, source_target_pairs={{0,4},{4,8},{8,12},{12,16},{16,20},{20,24},{24,28},{28,0},{1,5},{5... | collective-permute-start | bytes 245768 | tf_op jit(solution)/shard_map/ppermute | solution.py:40
  47.0 1.8 copy-start.3
  48.4 1.7 copy-start.2
  50.1 32.7 %copy-start.4 = (f32[320,64]{1,0:T(8,128)S(1)}, f32[320,64]{1,0:T(8,128)}, u32[]{:S(2)}) copy-start(f32[320,64]{1,0:T(8,128)} %get-tuple-element.279) | copy-start | bytes 245764
  50.1 32.7 %copy-start.5 = (f32[320,64]{1,0:T(8,128)S(1)}, f32[320,64]{1,0:T(8,128)}, u32[]{:S(2)}) copy-start(f32[320,64]{1,0:T(8,128)} %get-tuple-element.280) | copy-start | bytes 245764
  82.8 43.6 %copy-start.6 = (s32[4,5]{1,0:T(4,128)S(1)}, s32[4,5]{1,0:T(4,128)}, u32[]{:S(2)}) copy-start(s32[4,5]{1,0:T(4,128)} %param.17) | copy-start | bytes 244
  83.2 7.4 %collective-permute-start.1 = (bf16[320,1,128]{2,0,1:T(8,128)(2,1)}, bf16[320,1,128]{2,0,1:T(8,128)(2,1)S(1)}, u32[]{:S(2)}, u32[]{:S(2)}) collective-permute-start(bf16[320,1,128]{2,0,1:T(8,128)(2,1)} %collective-permute-done), channel_id=1, source_target_pairs={{0,4},{4,8},{8,12},{12,16},{16,20},{20,24},{24,28},{28,0},{1,5},{5... | collective-permute-start | bytes 245768 | tf_op jit(solution)/shard_map/ppermute | solution.py:40
  90.6 7.1 %collective-permute-start.2 = (bf16[320,1,128]{2,0,1:T(8,128)(2,1)S(1)}, bf16[320,1,128]{2,0,1:T(8,128)(2,1)S(1)}, u32[]{:S(2)}, u32[]{:S(2)}) collective-permute-start(bf16[320,1,128]{2,0,1:T(8,128)(2,1)S(1)} %collective-permute-done.1), channel_id=1, source_target_pairs={{0,4},{4,8},{8,12},{12,16},{16,20},{20,24},{24,28},{28,0},{1,5},{5... | collective-permute-start | bytes 245768 | tf_op jit(solution)/shard_map/ppermute | solution.py:40
  97.7 7.1 %collective-permute-start.3 = (bf16[320,1,128]{2,0,1:T(8,128)(2,1)S(1)}, bf16[320,1,128]{2,0,1:T(8,128)(2,1)S(1)}, u32[]{:S(2)}, u32[]{:S(2)}) collective-permute-start(bf16[320,1,128]{2,0,1:T(8,128)(2,1)S(1)} %collective-permute-done.2), channel_id=1, source_target_pairs={{0,4},{4,8},{8,12},{12,16},{16,20},{20,24},{24,28},{28,0},{1,5},{5... | collective-permute-start | bytes 245768 | tf_op jit(solution)/shard_map/ppermute | solution.py:40
  104.8 7.1 %collective-permute-start.4 = (bf16[320,1,128]{2,0,1:T(8,128)(2,1)S(1)}, bf16[320,1,128]{2,0,1:T(8,128)(2,1)S(1)}, u32[]{:S(2)}, u32[]{:S(2)}) collective-permute-start(bf16[320,1,128]{2,0,1:T(8,128)(2,1)S(1)} %collective-permute-done.3), channel_id=1, source_target_pairs={{0,4},{4,8},{8,12},{12,16},{16,20},{20,24},{24,28},{28,0},{1,5},{5... | collective-permute-start | bytes 245768 | tf_op jit(solution)/shard_map/ppermute | solution.py:40
  112.0 7.1 %collective-permute-start.5 = (bf16[320,1,128]{2,0,1:T(8,128)(2,1)S(1)}, bf16[320,1,128]{2,0,1:T(8,128)(2,1)S(1)}, u32[]{:S(2)}, u32[]{:S(2)}) collective-permute-start(bf16[320,1,128]{2,0,1:T(8,128)(2,1)S(1)} %collective-permute-done.4), channel_id=1, source_target_pairs={{0,4},{4,8},{8,12},{12,16},{16,20},{20,24},{24,28},{28,0},{1,5},{5... | collective-permute-start | bytes 245768 | tf_op jit(solution)/shard_map/ppermute | solution.py:40
  119.1 7.1 %collective-permute-start.6 = (bf16[320,1,128]{2,0,1:T(8,128)(2,1)S(1)}, bf16[320,1,128]{2,0,1:T(8,128)(2,1)S(1)}, u32[]{:S(2)}, u32[]{:S(2)}) collective-permute-start(bf16[320,1,128]{2,0,1:T(8,128)(2,1)S(1)} %collective-permute-done.5), channel_id=1, source_target_pairs={{0,4},{4,8},{8,12},{12,16},{16,20},{20,24},{24,28},{28,0},{1,5},{5... | collective-permute-start | bytes 245768 | tf_op jit(solution)/shard_map/ppermute | solution.py:40
Sparse Core Ops, SparseCore 0:
  8.9 28.2 all-gather.2
  142.7 47.3 reduce-scatter.1
